TPU v7x, 32 devices: a whole 2x2x4 slice. The times are simulated.
32 devices in a mesh: replica: 8 (over y, x, core), tok: 4 (over z).
Axes of the slice: x: 2, y: 2, z: 4, core: 2. Of those that a mesh axis runs over, the one named last changes fastest.
Arguments:
- activations: bfloat16 [8192, 2880], P(('replica', 'tok')), may hold values from -6 to 6
- cotangent: bfloat16 [8192, 512], P(('replica', 'tok')), may hold values from -6 to 6
- next_inputs: bfloat16 [8192, 2880], P(('replica', 'tok')), may hold values from -6 to 6
- weight_tiles: bfloat16 [360, 4096], P('tok'), may hold values from -0.109375 to 0.109375
- momentum: float32 [8, 360, 4096], P('replica', 'tok'), may hold values from -6 to 6
- chosen: int32 [8, 4, 8], P('replica', 'tok'), may hold values from 0 to 89, as said below
- counts: int32 [8, 4], P('replica', 'tok'), may hold values from 1 to 8, as said below
Outputs:
- values: bfloat16 [8192, 512], P(('replica', 'tok'))
- new_momentum: float32 [8, 360, 4096], P('replica', 'tok')
Inputs may be any that keep to these rules, and one draw needn't show every extreme that they name: Each list chosen[r, k] names 8 different tile numbers of the shard's 90 tiles; only the first counts[r, k] of them are selected. `counts`: in every draw some token shard has 8 selected tiles in every replica.
All inputs are finite; a program needn't handle non-finite values.
Results may differ from a plain program's by a relative error of at most 0.015.
Values may be sent and summed in bfloat16 or wider, within the bound.
No kernel may reach another device: no remote copies, remote signals or barrier semaphores. Data moves between devices by JAX's collectives and lax.ppermute only.
A program may use at most 64 MiB of HBM per device.

v0:
```python
import math
import jax
import jax.numpy as jnp
from jax import lax
from jax.sharding import PartitionSpec as P

TILE = 64
KEEP = 32
momentum_decay = 0.9
step_size = 0.01


def cosine_rows(count):
    frequency = jnp.arange(count, dtype=jnp.float32)[:, None]
    position = jnp.arange(TILE, dtype=jnp.float32)[None, :]
    cosines = jnp.cos(math.pi * (2.0 * position + 1.0) * frequency / (2.0 * TILE))
    factor = jnp.where(frequency == 0, math.sqrt(1.0 / TILE), math.sqrt(2.0 / TILE))
    return cosines * factor


def rebuild(summed, weight_part, keep_rows):
    quads = summed.reshape(summed.shape[0], KEEP, KEEP)
    update = jnp.einsum(
        "ua,tuv,vb->tab", keep_rows, quads, keep_rows, precision=lax.Precision.HIGHEST
    )
    shifted = weight_part.astype(jnp.float32) - step_size * update.reshape(
        summed.shape[0], TILE * TILE
    )
    return shifted.astype(jnp.bfloat16)


def forward(inputs, new_tiles):
    row_tiles = inputs.shape[1] // TILE
    col_tiles = new_tiles.shape[0] // row_tiles
    blocks = inputs.reshape(inputs.shape[0], row_tiles, TILE)
    matrix = new_tiles.reshape(row_tiles, col_tiles, TILE, TILE)
    output = jnp.einsum("tra,rcab->tcb", blocks, matrix, preferred_element_type=jnp.float32)
    return output.reshape(inputs.shape[0], col_tiles * TILE).astype(jnp.bfloat16)


def local(activations, cotangent, next_inputs, weight_tiles, momentum, chosen, counts):
    highest = lax.Precision.HIGHEST
    shards = lax.axis_size("tok")
    tiles_here = weight_tiles.shape[0]
    row_tiles = activations.shape[1] // TILE
    col_tiles = cotangent.shape[1] // TILE
    grad_scale = 1.0 / math.sqrt(activations.shape[0] * shards)
    keep_rows = cosine_rows(KEEP)
    row_span = min(tiles_here * lax.axis_size("tok") // col_tiles + 2, row_tiles)
    product = (
        lax.dot_general(
            activations, cotangent, (((0,), (0,)), ((), ())), preferred_element_type=jnp.float32
        )
        * grad_scale
    )
    tiled = product.reshape(row_span, TILE, col_tiles, TILE).transpose(0, 2, 1, 3)
    tiled = tiled.reshape(row_span * col_tiles, TILE * TILE)
    gradient = lax.psum_scatter(
        tiled.astype(jnp.bfloat16), "tok", scatter_dimension=0, tiled=True
    ).astype(jnp.float32)
    updated = momentum_decay * momentum[0] + gradient
    chosen_here = chosen[0, 0]
    in_list = jnp.arange(chosen_here.shape[0], dtype=jnp.int32) < counts[0, 0]
    picked = jnp.take(updated, chosen_here, axis=0).reshape(-1, TILE, TILE)
    quadrant = jnp.einsum("ua,nab,vb->nuv", keep_rows, picked, keep_rows, precision=highest)
    quadrant = jnp.where(in_list[:, None, None], quadrant, 0.0).astype(jnp.bfloat16)
    rebuilt = jnp.einsum(
        "ua,nuv,vb->nab", keep_rows, quadrant.astype(jnp.float32), keep_rows, precision=highest
    )
    new_momentum = updated.at[chosen_here].add(-rebuilt.reshape(-1, TILE * TILE))
    listed = jnp.where(in_list, chosen_here, -1)
    flat_quads = quadrant.reshape(-1, KEEP * KEEP)
    tile_numbers = jnp.arange(tiles_here, dtype=jnp.int32)
    all_quads, all_listed = (
        lax.all_gather(flat_quads, "replica", axis=0, tiled=True),
        lax.all_gather(listed, "replica", axis=0, tiled=True),
    )
    one_hot = (all_listed[:, None] == tile_numbers[None, :]).astype(jnp.bfloat16)
    summed = lax.dot_general(
        one_hot, all_quads, (((0,), (0,)), ((), ())), preferred_element_type=jnp.float32
    )
    new_part = rebuild(summed, weight_tiles, keep_rows)
    new_full = lax.all_gather(new_part, "tok", axis=0, tiled=True)
    values = forward(next_inputs, new_full)
    return (values, new_momentum[None])


def solution(mesh):
    return jax.shard_map(
        local,
        mesh=mesh,
        in_specs=(
            P(("replica", "tok"), None),
            P(("replica", "tok"), None),
            P(("replica", "tok"), None),
            P("tok", None),
            P("replica", "tok", None),
            P("replica", "tok", None),
            P("replica", "tok"),
        ),
        out_specs=(P(("replica", "tok"), None), P("replica", "tok", None)),
        check_vma=False,
    )
```

profile of v0, /device:TPU:0, one launch (start us, length us, event | category | flops | bytes accessed | tf_op | source)
XLA Modules:
  0.0 222.4 jit_solution(13789088672530609271)
XLA Ops:
  7.2 1.3 copy-done
  8.5 3.5 %multiply_convert_fusion = bf16[2880,512]{1,0:T(8,128)(2,1)} fusion(bf16[256,2880]{0,1:T(8,128)(2,1)S(1)} %copy-done, bf16[256,512]{1,0:T(8,128)(2,1)} %param.8), kind=kOutput, calls=%fused_computation.2 | convolution fusion | flops 757923840 | bytes 4685824 | tf_op jit(solution)/shard_map/dot_general | solution.py:51
  12.1 8.4 %convert_element_type.37 = bf16[45,64,8,64]{3,2,1,0:T(8,128)(2,1)} reshape(bf16[2880,512]{1,0:T(8,128)(2,1)} %multiply_convert_fusion) | data formatting | bytes 5898240 | tf_op jit(solution)/shard_map/convert_element_type | solution.py:59
  20.5 7.0 %copy.22 = bf16[45,8,64,64]{3,2,1,0:T(8,128)(2,1)} copy(bf16[45,8,64,64]{3,1,2,0:T(8,128)(2,1)} %bitcast.59) | data formatting | bytes 5898240 | tf_op jit(solution)/shard_map/convert_element_type | solution.py:59
  27.5 8.7 %convert_element_type.39 = bf16[360,4096]{1,0:T(8,128)(2,1)} reshape(bf16[45,8,64,64]{3,2,1,0:T(8,128)(2,1)} %copy.22) | data formatting | bytes 5898240 | tf_op jit(solution)/shard_map/convert_element_type | solution.py:59
  36.2 61.9 %fusion = bf16[96,4096]{1,0:T(8,128)(2,1)S(1)} fusion(bf16[360,4096]{1,0:T(8,128)(2,1)} %convert_element_type.39), kind=kCustom, calls=%all-reduce-scatter | all-reduce-scatter fusion | flops 1572865 | bytes 3736064
  98.2 1.7 collective-permute-start
  100.6 0.6 dynamic-slice
  102.0 0.6 dynamic-slice.5
  103.2 8.0 %all-reduce = s32[64]{0:T(128)S(1)} all-reduce(s32[64]{0:T(128)S(1)} %fusion.39), channel_id=1, replica_groups=mesh['replica'=8,'tok'=4] {'replica'}, use_global_device_ids=true, to_apply=%add | all-reduce | flops 64 | bytes 512
  111.3 5.8 %concatenate = bf16[114,4096]{1,0:T(8,128)(2,1)} concatenate(bf16[18,4096]{1,0:T(8,128)(2,1)S(1)} %collective-permute-done, bf16[96,4096]{1,0:T(8,128)(2,1)S(1)} %fusion), dimensions={0} | concatenate | bytes 1867776
  117.1 2.9 %bitcast_add_fusion = f32[90,4096]{1,0:T(8,128)S(1)} fusion(f32[1,90,4096]{2,0,1:T(1,128)} %param.11, bf16[114,4096]{1,0:T(8,128)(2,1)} %concatenate, u32[]{:S(6)} %subtract), kind=kLoop, calls=%fused_computation.4 | loop fusion | flops 1105920 | bytes 3686404 | tf_op jit(solution)/shard_map/add | solution.py:61
  119.9 0.6 gather_fusion
  120.5 0.1 gather.7
  120.6 0.4 fusion.7
  121.0 0.3 fusion.2
  121.3 0.1 reshape.90
  121.5 8.7 %all_gather.10 = bf16[64,1024]{1,0:T(8,128)(2,1)S(1)} all-gather(bf16[8,1024]{1,0:T(8,128)(2,1)S(1)} %reshape.90), channel_id=1, replica_groups=mesh['replica'=8,'tok'=4] {'replica'}, dimensions={0}, use_global_device_ids=true | all-gather | bytes 147456 | tf_op jit(solution)/shard_map/all_gather | solution.py:75
  130.2 0.3 fusion.11
  130.5 1.4 fusion.5
  131.9 3.9 %convolution_multiply_fusion = f32[90,64,64]{0,2,1:T(8,128)} fusion(f32[90,32,64]{0,2,1:T(8,128)S(1)} %fusion.5, f32[32]{0:T(128)S(1)} %compare_select_fusion.2, f32[64]{0:T(128)S(1)} %add_multiply_fusion), kind=kOutput, calls=%fused_computation.3 | convolution fusion | flops 141932544 | bytes 2212224 | tf_op jit(solution)/shard_map/ua,tuv,vb->tab/dot_general | solution.py:23
  135.8 2.8 %copy.26 = f32[90,4096]{1,0:T(8,128)} copy(f32[90,4096]{0,1:T(8,128)} %bitcast.61) | data formatting | bytes 2949120 | tf_op jit(solution)/shard_map/mul | solution.py:26
  138.6 2.6 %fusion.4 = bf16[1,90,4096]{2,1,0:T(8,128)(2,1)} fusion(f32[90,4096]{1,0:T(8,128)} %copy.26, bf16[90,4096]{1,0:T(8,128)(2,1)} %param.10), kind=kLoop, calls=%fused_computation.13 | loop fusion | flops 1105920 | bytes 2949120
  141.3 0.3 fusion.13
  141.6 0.6 convolution_negate_fusion
  142.2 0.1 reshape.106
  142.3 1.3 scatter_fusion
  143.7 2.6 %copy.30 = f32[1,90,4096]{2,0,1:T(1,128)} copy(f32[1,90,4096]{2,1,0:T(8,128)S(1)} %bitcast.60) | data formatting | bytes 2949120
  146.3 55.8 %all-gather.3.cloned.1.call-done = bf16[4,90,4096]{2,1,0:T(8,128)(2,1)} async-done(((bf16[1,90,4096]{2,1,0:T(8,128)(2,1)}), bf16[4,90,4096]{2,1,0:T(8,128)(2,1)}) %all-gather.3.cloned.1.call-update) | async-done | bytes 2949136 | tf_op jit(solution)/shard_map/all_gather | solution.py:83
  202.1 8.2 %reshape.92 = bf16[45,8,64,64]{3,2,1,0:T(8,128)(2,1)} reshape(bf16[4,90,4096]{2,1,0:T(8,128)(2,1)} %all-gather.3.cloned.1.call-done) | data formatting | bytes 5898240 | tf_op jit(solution)/shard_map/reshape | solution.py:36
  210.2 4.4 %fusion.1 = bf16[8,64,256]{2,1,0:T(8,128)(2,1)S(1)} fusion(bf16[45,8,64,64]{3,2,1,0:T(8,128)(2,1)} %reshape.92, bf16[256,45,64,1]{0,2,3,1:T(8,128)(2,1)S(1)} %bitcast.63), kind=kOutput, calls=%fused_computation.8 | convolution fusion | flops 755105792 | bytes 4685824 | tf_op jit(solution)/shard_map/tra,rcab->tcb/dot_general | solution.py:37
  214.7 0.8 copy.29
  (21 shorter events, 0.3 us)
Async XLA Ops:
  7.2 1.4 copy-start
  7.2 194.9 %all-gather.3.cloned.1.call-start = ((), (), s32[]{:S(2)}) async-start(), calls=%async_computation | async-start | bytes 3932160 | tf_op jit(solution)/shard_map/all_gather | solution.py:83
  36.2 63.7 %copy-start.3 = (s32[1,1,8]{2,1,0:T(1,128)S(1)}, s32[1,1,8]{2,1,0:T(1,128)}, u32[]{:S(2)}) copy-start(s32[1,1,8]{2,1,0:T(1,128)} %param.12) | copy-start | bytes 100
  36.2 64.4 %copy-start.4 = (u32[32]{0:T(128)S(1)}, u32[32]{0:T(128)}, u32[]{:S(2)}) copy-start(u32[32]{0:T(128)} %constant.48) | copy-start | bytes 388
  36.2 65.8 %copy-start.2 = (u32[32]{0:T(128)S(1)}, u32[32]{0:T(128)}, u32[]{:S(2)}) copy-start(u32[32]{0:T(128)} %constant.54) | copy-start | bytes 388
  98.2 13.1 %collective-permute-start = (bf16[18,4096]{1,0:T(8,128)(2,1)S(1)}, bf16[18,4096]{1,0:T(8,128)(2,1)S(1)}, u32[]{:S(2)}, u32[]{:S(2)}) collective-permute-start(bf16[18,4096]{1,0:T(8,128)(2,1)S(1)} %slice.2), channel_id=1, source_target_pairs={{0,1},{1,2},{2,3},{4,5},{5,6},{6,7},{8,9},{9,10},{10,11},{12,13},{... | collective-permute-start | bytes 442376
  146.3 64.0 %copy-start.1 = (bf16[256,2880]{0,1:T(8,128)(2,1)S(1)}, bf16[256,2880]{0,1:T(8,128)(2,1)}, u32[]{:S(2)}) copy-start(bf16[256,2880]{0,1:T(8,128)(2,1)} %param.9) | copy-start | bytes 4423684
Sparse Core Ops, SparseCore 0:
  141.4 60.6 all-gather.2
where the time goes:
time: 224 us; the launch traced here: 222 us
  blocking collectives  78.7 us (35%)
  waiting for transfers between devices  55.8 us (25%)
  local copies, waits for them, and re-layouts  47.9 us (21%)
  between operations  16.2 us (7%)
  matrix products  15.1 us (7%)
  other arithmetic  6.99 us (3%)
    unnamed x2, blocking collectives  69.9 us
    all_gather x1, waiting for transfers between devices, local(): new_full = lax.all_gather(new_part, 'tok', axis=0, tiled=True)  55.8 us
    convert_element_type x3, local copies, waits for them, and re-layouts, local(): tiled.astype(jnp.bfloat16)  24.1 us
    unnamed x17, local copies, waits for them, and re-layouts  11.9 us
    all_gather x1, blocking collectives, local(): lax.all_gather(flat_quads, 'replica', axis=0, tiled=True)  8.73 us
    reshape x1, local copies, waits for them, and re-layouts, forward(): matrix = new_tiles.reshape(row_tiles, col_tiles, TILE, TILE)  8.17 us
    dot_general x2, matrix products, rebuild(): jnp.einsum('ua,tuv,vb->tab', keep_rows, quads, keep_rows, precision=lax.P...  5.25 us
  transfers between devices with their start and end apart: 2, of which 1 were waited for; matrix products, arithmetic and copies ran while one was open for 3% of the time, Pallas kernels for 0%

commit v1 on v0

--- a/solution.py
+++ b/solution.py
@@ -8,6 +8,34 @@
 KEEP = 32
 momentum_decay = 0.9
 step_size = 0.01
+
+
+def write_units(array_in, axis_no):
+    array_in = jnp.moveaxis(array_in, 0, axis_no)
+    current_value = array_in.shape
+    opened = array_in.reshape(
+        *current_value[:axis_no],
+        current_value[axis_no] * current_value[axis_no + 1],
+        *current_value[axis_no + 2 :]
+    )
+    return opened
+
+
+def clear_sections(block_in, axis_id, array_axis=0):
+    amount_of = lax.axis_size(axis_id)
+    seen = [(no, (no + 1) % amount_of) for no in range(amount_of)]
+    f_next, front = ([], [])
+    column = [(to_i, d) for d, to_i in seen]
+    for it in range(amount_of - 1):
+        if it % 2 == 0:
+            f_next.append(lax.ppermute(f_next[-1] if f_next else block_in, axis_id, seen))
+        else:
+            front.append(lax.ppermute(front[-1] if front else block_in, axis_id, column))
+    local_next = jnp.stack([*f_next[::-1], block_in, *front])
+    spare = lax.axis_index(axis_id) - len(f_next)
+    local_next = local_next[(jnp.arange(amount_of) - spare) % amount_of]
+    aux = write_units(local_next, array_axis)
+    return aux
 
 
 def cosine_rows(count):
@@ -80,7 +108,7 @@
         one_hot, all_quads, (((0,), (0,)), ((), ())), preferred_element_type=jnp.float32
     )
     new_part = rebuild(summed, weight_tiles, keep_rows)
-    new_full = lax.all_gather(new_part, "tok", axis=0, tiled=True)
+    new_full = clear_sections(new_part, "tok")
     values = forward(next_inputs, new_full)
     return (values, new_momentum[None])
 

time: 224 us -> 213 us (0.951)
  between operations: 16.2 us -> 2.77 us
  waiting for transfers between devices: 55.8 us -> 46.8 us
  local copies, waits for them, and re-layouts: 47.9 us -> 52.4 us
  starting transfers between devices: 1.74 us -> 5.53 us
  other arithmetic: 6.99 us -> 10.5 us
    all_gather x1 -> x0, waiting for transfers between devices: 55.8 us -> none  [local(): new_full = lax.all_gather(new_part, 'tok', axis=0, tiled=True)]
    ppermute x0 -> x3, waiting for transfers between devices: none -> 46.8 us  [the longest x2 37.4 us: clear_sections(): lax.ppermute(f_next[-1] if f_next else block_in, axis_id, seen)]
    another operation x0 -> x1, local copies, waits for them, and re-layouts: none -> 8.28 us  [forward(): matrix = new_tiles.reshape(row_tiles, col_tiles, TILE, TILE)]
    reshape x1 -> x0, local copies, waits for them, and re-layouts: 8.17 us -> none  [forward(): matrix = new_tiles.reshape(row_tiles, col_tiles, TILE, TILE)]
    gather x0 -> x1, local copies, waits for them, and re-layouts: none -> 4.35 us  [clear_sections(): local_next = local_next[(jnp.arange(amount_of) - spare) % amount_of]]
    ppermute x0 -> x3, starting transfers between devices: none -> 3.83 us  [the longest x1 3.49 us: clear_sections(): lax.ppermute(front[-1] if front else block_in, axis_id, column)]
    another operation x0 -> x1, other arithmetic: none -> 3.44 us  [clear_sections(): local_next = jnp.stack([*f_next[::-1], block_in, *front])]
    convert_element_type x0 -> x1, other arithmetic: none -> 2.65 us  [rebuild(): return shifted.astype(jnp.bfloat16)]
  transfers between devices with their start and end apart: 2 -> 4, of which waited for: 1 -> 3; matrix products, arithmetic and copies ran while one was open for 3% -> 3% of each run, Pallas kernels for 0% -> 0%
where the time goes in v1:
time: 213 us; the launch traced here: 212 us
  blocking collectives  78.5 us (37%)
  local copies, waits for them, and re-layouts  52.4 us (25%)
  waiting for transfers between devices  46.8 us (22%)
  matrix products  15.1 us (7%)
  other arithmetic  10.5 us (5%)
  starting transfers between devices  5.53 us (3%)
  between operations  2.77 us (1%)
    unnamed x2, blocking collectives  69.9 us
    ppermute x2, waiting for transfers between devices, clear_sections(): lax.ppermute(f_next[-1] if f_next else block_in, axis_id, seen)  37.4 us
    convert_element_type x3, local copies, waits for them, and re-layouts, local(): tiled.astype(jnp.bfloat16)  24.1 us
    unnamed x17, local copies, waits for them, and re-layouts  11.9 us
    ppermute x1, waiting for transfers between devices, clear_sections(): lax.ppermute(front[-1] if front else block_in, axis_id, column)  9.37 us
    all_gather x1, blocking collectives, local(): lax.all_gather(flat_quads, 'replica', axis=0, tiled=True)  8.55 us
    another operation x1, local copies, waits for them, and re-layouts, forward(): matrix = new_tiles.reshape(row_tiles, col_tiles, TILE, TILE)  8.28 us
    dot_general x2, matrix products, rebuild(): jnp.einsum('ua,tuv,vb->tab', keep_rows, quads, keep_rows, precision=lax.P...  5.25 us
  transfers between devices with their start and end apart: 4, of which 3 were waited for; matrix products, arithmetic and copies ran while one was open for 3% of the time, Pallas kernels for 0%

profile of v1, /device:TPU:0, one launch (start us, length us, event | category | flops | bytes accessed | tf_op | source)
XLA Modules:
  0.0 211.6 jit_solution(5993817045334967657)
XLA Ops:
  0.6 1.4 copy-done
  2.0 3.5 %multiply_convert_fusion = bf16[2880,512]{1,0:T(8,128)(2,1)} fusion(bf16[256,2880]{0,1:T(8,128)(2,1)S(1)} %copy-done, bf16[256,512]{1,0:T(8,128)(2,1)} %param.8), kind=kOutput, calls=%fused_computation.3 | convolution fusion | flops 757923840 | bytes 4685824 | tf_op jit(solution)/shard_map/dot_general | solution.py:79
  5.5 8.4 %convert_element_type.37 = bf16[45,64,8,64]{3,2,1,0:T(8,128)(2,1)} reshape(bf16[2880,512]{1,0:T(8,128)(2,1)} %multiply_convert_fusion) | data formatting | bytes 5898240 | tf_op jit(solution)/shard_map/convert_element_type | solution.py:87
  13.9 7.0 %copy.23 = bf16[45,8,64,64]{3,2,1,0:T(8,128)(2,1)} copy(bf16[45,8,64,64]{3,1,2,0:T(8,128)(2,1)} %bitcast.63) | data formatting | bytes 5898240 | tf_op jit(solution)/shard_map/convert_element_type | solution.py:87
  20.9 8.7 %convert_element_type.39 = bf16[360,4096]{1,0:T(8,128)(2,1)} reshape(bf16[45,8,64,64]{3,2,1,0:T(8,128)(2,1)} %copy.23) | data formatting | bytes 5898240 | tf_op jit(solution)/shard_map/convert_element_type | solution.py:87
  29.7 61.9 %fusion = bf16[96,4096]{1,0:T(8,128)(2,1)S(1)} fusion(bf16[360,4096]{1,0:T(8,128)(2,1)} %convert_element_type.39), kind=kCustom, calls=%all-reduce-scatter | all-reduce-scatter fusion | flops 1572865 | bytes 3736064
  91.6 1.7 collective-permute-start.3
  94.1 0.6 dynamic-slice
  95.4 0.6 dynamic-slice.5
  96.7 8.0 %all-reduce = s32[64]{0:T(128)S(1)} all-reduce(s32[64]{0:T(128)S(1)} %fusion.40), channel_id=1, replica_groups=mesh['replica'=8,'tok'=4] {'replica'}, use_global_device_ids=true, to_apply=%add | all-reduce | flops 64 | bytes 512
  104.7 5.8 %concatenate = bf16[114,4096]{1,0:T(8,128)(2,1)} concatenate(bf16[18,4096]{1,0:T(8,128)(2,1)S(1)} %collective-permute-done.3, bf16[96,4096]{1,0:T(8,128)(2,1)S(1)} %fusion), dimensions={0} | concatenate | bytes 1867776
  110.5 2.9 %bitcast_add_fusion = f32[90,4096]{1,0:T(8,128)S(1)} fusion(f32[1,90,4096]{2,0,1:T(1,128)} %param.11, bf16[114,4096]{1,0:T(8,128)(2,1)} %concatenate, u32[]{:S(6)} %subtract), kind=kLoop, calls=%fused_computation.6 | loop fusion | flops 1105920 | bytes 3686404 | tf_op jit(solution)/shard_map/add | solution.py:89
  113.4 0.6 gather_fusion
  114.1 0.4 fusion.6
  114.9 8.5 %all_gather.7 = bf16[64,1024]{1,0:T(8,128)(2,1)S(1)} all-gather(bf16[8,1024]{1,0:T(8,128)(2,1)S(1)} %reshape.136), channel_id=1, replica_groups=mesh['replica'=8,'tok'=4] {'replica'}, dimensions={0}, use_global_device_ids=true | all-gather | bytes 147456 | tf_op jit(solution)/shard_map/all_gather | solution.py:103
  123.8 1.4 fusion.4
  125.2 3.9 %convolution_multiply_fusion = f32[90,64,64]{0,2,1:T(8,128)} fusion(f32[90,32,64]{0,2,1:T(8,128)S(1)} %fusion.4, f32[32]{0:T(128)S(1)} %compare_select_fusion.5, f32[64]{0:T(128)S(1)} %add_multiply_fusion), kind=kOutput, calls=%fused_computation.5 | convolution fusion | flops 141932544 | bytes 2212224 | tf_op jit(solution)/shard_map/ua,tuv,vb->tab/dot_general | solution.py:51
  129.0 2.8 %copy.27 = f32[90,4096]{1,0:T(8,128)} copy(f32[90,4096]{0,1:T(8,128)} %bitcast.65) | data formatting | bytes 2949120 | tf_op jit(solution)/shard_map/mul | solution.py:54
  131.9 2.7 %subtract_convert_fusion = bf16[90,4096]{1,0:T(8,128)(2,1)} fusion(f32[90,4096]{1,0:T(8,128)} %copy.27, bf16[90,4096]{1,0:T(8,128)(2,1)} %param.10), kind=kLoop, calls=%fused_computation.8 | loop fusion | flops 1105920 | bytes 2949120 | tf_op jit(solution)/shard_map/convert_element_type | solution.py:57
  134.5 0.3 collective-permute-start
  134.9 3.5 %collective-permute-start.2 = (bf16[90,4096]{1,0:T(8,128)(2,1)}, bf16[90,4096]{1,0:T(8,128)(2,1)}, u32[]{:S(2)}, u32[]{:S(2)}) collective-permute-start(bf16[90,4096]{1,0:T(8,128)(2,1)} %subtract_convert_fusion), channel_id=1, source_target_pairs={{1,0},{2,1},{3,2},{0,3},{5,4},{6,5},{7,6},{4,7},{9,8},{10,9},{11,1... | collective-permute-start | bytes 2211848 | tf_op jit(solution)/shard_map/ppermute | solution.py:33
  138.4 18.8 %collective-permute-done = bf16[90,4096]{1,0:T(8,128)(2,1)} collective-permute-done((bf16[90,4096]{1,0:T(8,128)(2,1)}, bf16[90,4096]{1,0:T(8,128)(2,1)}, u32[]{:S(2)}, u32[]{:S(2)}) %collective-permute-start) | collective-permute-done | bytes 737312 | tf_op jit(solution)/shard_map/ppermute | solution.py:31
  157.4 0.6 convolution_negate_fusion
  158.2 1.3 scatter_fusion
  159.6 2.6 %copy.31 = f32[1,90,4096]{2,0,1:T(1,128)} copy(f32[1,90,4096]{2,1,0:T(8,128)S(1)} %bitcast.64) | data formatting | bytes 2949120
  162.2 9.4 %collective-permute-done.2 = bf16[90,4096]{1,0:T(8,128)(2,1)} collective-permute-done((bf16[90,4096]{1,0:T(8,128)(2,1)}, bf16[90,4096]{1,0:T(8,128)(2,1)}, u32[]{:S(2)}, u32[]{:S(2)}) %collective-permute-start.2) | collective-permute-done | bytes 737312 | tf_op jit(solution)/shard_map/ppermute | solution.py:33
  171.6 18.6 %collective-permute-done.1 = bf16[90,4096]{1,0:T(8,128)(2,1)} collective-permute-done((bf16[90,4096]{1,0:T(8,128)(2,1)}, bf16[90,4096]{1,0:T(8,128)(2,1)}, u32[]{:S(2)}, u32[]{:S(2)}) %collective-permute-start.1) | collective-permute-done | bytes 737312 | tf_op jit(solution)/shard_map/ppermute | solution.py:31
  190.2 3.4 %pad_maximum_fusion = bf16[4,90,4096]{2,1,0:T(8,128)(2,1)} fusion(bf16[1,90,4096]{2,1,0:T(8,128)(2,1)} %bitcast.13, bf16[1,90,4096]{2,1,0:T(8,128)(2,1)} %bitcast.12, bf16[1,90,4096]{2,1,0:T(8,128)(2,1)} %bitcast.11, bf16[1,90,4096]{2,1,0:T(8,128)(2,1)} %bitcast.10), kind=kLoop, calls=%fused_computation.4 | loop fusion | flops 4423680 | bytes 5898240 | tf_op jit(solution)/shard_map/stack | solution.py:34
  193.6 4.3 %gather_fusion.1 = bf16[4,90,4096]{2,1,0:T(8,128)(2,1)} fusion(bf16[4,90,4096]{2,1,0:T(8,128)(2,1)} %pad_maximum_fusion, s32[1024]{0:T(1024)S(1)} %pad_clamp_fusion), kind=kCustom, calls=%fused_computation.1 | custom fusion | bytes 5898256 | tf_op jit(solution)/shard_map/gather | solution.py:36
  198.0 8.3 %reshape_reshape.3 = bf16[45,8,64,64]{3,2,1,0:T(8,128)(2,1)} reshape(bf16[4,90,4096]{2,1,0:T(8,128)(2,1)} %gather_fusion.1) | data formatting | bytes 5898240 | tf_op jit(solution)/shard_map/reshape;reshape | solution.py:64
  206.3 4.4 %fusion.1 = bf16[8,64,256]{2,1,0:T(8,128)(2,1)S(1)} fusion(bf16[45,8,64,64]{3,2,1,0:T(8,128)(2,1)} %reshape_reshape.3, bf16[256,45,64,1]{0,2,3,1:T(8,128)(2,1)S(1)} %bitcast.67), kind=kOutput, calls=%fused_computation.10 | convolution fusion | flops 755105792 | bytes 4685824 | tf_op jit(solution)/shard_map/tra,rcab->tcb/dot_general | solution.py:65
  210.7 0.8 copy.30
  (28 shorter events, 1.5 us)
Async XLA Ops:
  0.6 1.4 copy-start
  29.7 63.7 %copy-start.3 = (s32[1,1,8]{2,1,0:T(1,128)S(1)}, s32[1,1,8]{2,1,0:T(1,128)}, u32[]{:S(2)}) copy-start(s32[1,1,8]{2,1,0:T(1,128)} %param.12) | copy-start | bytes 100
  29.7 64.4 %copy-start.4 = (u32[32]{0:T(128)S(1)}, u32[32]{0:T(128)}, u32[]{:S(2)}) copy-start(u32[32]{0:T(128)} %constant.71) | copy-start | bytes 388
  29.7 65.8 %copy-start.2 = (u32[32]{0:T(128)S(1)}, u32[32]{0:T(128)}, u32[]{:S(2)}) copy-start(u32[32]{0:T(128)} %constant.77) | copy-start | bytes 388
  91.6 13.1 %collective-permute-start.3 = (bf16[18,4096]{1,0:T(8,128)(2,1)S(1)}, bf16[18,4096]{1,0:T(8,128)(2,1)S(1)}, u32[]{:S(2)}, u32[]{:S(2)}) collective-permute-start(bf16[18,4096]{1,0:T(8,128)(2,1)S(1)} %slice.4), channel_id=1, source_target_pairs={{0,1},{1,2},{2,3},{4,5},{5,6},{6,7},{8,9},{9,10},{10,11},{12,13},{... | collective-permute-start | bytes 442376
  134.5 22.6 %collective-permute-start = (bf16[90,4096]{1,0:T(8,128)(2,1)}, bf16[90,4096]{1,0:T(8,128)(2,1)}, u32[]{:S(2)}, u32[]{:S(2)}) collective-permute-start(bf16[90,4096]{1,0:T(8,128)(2,1)} %subtract_convert_fusion), channel_id=1, source_target_pairs={{0,1},{1,2},{2,3},{3,0},{4,5},{5,6},{6,7},{7,4},{8,9},{9,10},{10,1... | collective-permute-start | bytes 2211848 | tf_op jit(solution)/shard_map/ppermute | solution.py:31
  134.9 36.7 %collective-permute-start.2 = (bf16[90,4096]{1,0:T(8,128)(2,1)}, bf16[90,4096]{1,0:T(8,128)(2,1)}, u32[]{:S(2)}, u32[]{:S(2)}) collective-permute-start(bf16[90,4096]{1,0:T(8,128)(2,1)} %subtract_convert_fusion), channel_id=1, source_target_pairs={{1,0},{2,1},{3,2},{0,3},{5,4},{6,5},{7,6},{4,7},{9,8},{10,9},{11,1... | collective-permute-start | bytes 2211848 | tf_op jit(solution)/shard_map/ppermute | solution.py:33
  157.1 33.1 %collective-permute-start.1 = (bf16[90,4096]{1,0:T(8,128)(2,1)}, bf16[90,4096]{1,0:T(8,128)(2,1)}, u32[]{:S(2)}, u32[]{:S(2)}) collective-permute-start(bf16[90,4096]{1,0:T(8,128)(2,1)} %collective-permute-done), channel_id=1, source_target_pairs={{0,1},{1,2},{2,3},{3,0},{4,5},{5,6},{6,7},{7,4},{8,9},{9,10},{10,1... | collective-permute-start | bytes 2211848 | tf_op jit(solution)/shard_map/ppermute | solution.py:31
  198.0 8.3 %copy-start.1 = (bf16[256,2880]{0,1:T(8,128)(2,1)S(1)}, bf16[256,2880]{0,1:T(8,128)(2,1)}, u32[]{:S(2)}) copy-start(bf16[256,2880]{0,1:T(8,128)(2,1)} %param.9) | copy-start | bytes 4423684
